TPU v7x, 32 devices: a whole 2x2x4 slice. The times are simulated.
32 devices in a mesh: space: 8 (over y, x, core), tm: 4 (over z).
Axes of the slice: x: 2, y: 2, z: 4, core: 2. Of those that a mesh axis runs over, the one named last changes fastest.
Arguments:
- series: bfloat16 [16384, 2, 512], P('space', None, 'tm'), may hold values from -6 to 6
- space_basis: bfloat16 [16384, 16384], P('space', 'tm'), may hold values from -0.046875 to 0.046875
- time_basis: bfloat16 [512, 512], P('tm'), may hold values from -0.25 to 0.25
- space_eig: float32 [16384], replicated, may hold values from 0.3 to 3
- time_eig: float32 [512], replicated, may hold values from 0.3 to 3
Outputs:
- alpha: bfloat16 [16384, 2, 512], P('space', None, 'tm')
- grad_space: bfloat16 [16384, 8, 2048], P('space', None, 'tm')
All inputs are finite; a program needn't handle non-finite values.
Results may differ from a plain program's by a relative error of at most 0.0063.
Values may be sent and summed in bfloat16 or wider, within the bound.
A program may use at most 128 MiB of HBM per device.

v0:
```python
import jax
import jax.numpy as jnp
from jax import lax
from jax.sharding import PartitionSpec as P

TIMES = 512
REPS = 2


def scale_block(spectral, eig_rows, eig_cols):
    denom = eig_rows[:, None] * eig_cols[None, :] + 0.1
    return (spectral / denom).astype(jnp.bfloat16)


def per_device(series, space_basis, time_basis, space_eig, time_eig):
    space_count = lax.axis_size("space")
    time_count = lax.axis_size("tm")
    time_idx = lax.axis_index("tm")
    row_count = space_basis.shape[0]
    col_block = space_basis.shape[1]
    time_local = time_basis.shape[0]
    wide_cols = REPS * TIMES
    sub_rows = row_count // time_count
    cols_tiled = jnp.tile(time_eig, REPS)
    full_series, full_basis = (
        lax.all_gather(series, "tm", axis=2, tiled=True),
        lax.all_gather(time_basis, "tm", axis=0, tiled=True),
    )
    rotated = jnp.dot(
        full_series.reshape(row_count * REPS, TIMES), full_basis, preferred_element_type=jnp.float32
    ).astype(jnp.bfloat16)
    rotated = rotated.reshape(row_count, wide_cols)
    contract_rows = (((0,), (0,)), ((), ()))
    partial_spec = lax.dot_general(
        space_basis, rotated, contract_rows, preferred_element_type=jnp.float32
    )
    spectral = lax.psum(partial_spec, "space")
    eig_rows = lax.dynamic_slice_in_dim(space_eig, time_idx * col_block, col_block)
    scaled_spec = scale_block(spectral, eig_rows, cols_tiled)
    back_part = jnp.dot(space_basis, scaled_spec, preferred_element_type=jnp.float32)
    back_all = lax.psum(back_part, "tm").astype(jnp.bfloat16)
    back_sub = lax.dynamic_slice_in_dim(back_all, time_idx * sub_rows, sub_rows, 0)
    contract_last = (((1,), (1,)), ((), ()))
    alpha = lax.dot_general(
        back_all.reshape(row_count * REPS, TIMES),
        time_basis,
        contract_last,
        preferred_element_type=jnp.float32,
    )
    alpha = alpha.astype(jnp.bfloat16).reshape(row_count, REPS, time_local)
    weighted = (
        back_all.reshape(row_count, REPS, TIMES).astype(jnp.float32) * time_eig[None, None, :]
    )
    weighted = (weighted / (REPS * TIMES)).astype(jnp.bfloat16).reshape(row_count, wide_cols)
    grad = lax.dot_general(
        weighted,
        lax.all_gather(back_sub, "space", axis=0, tiled=True),
        contract_last,
        preferred_element_type=jnp.float32,
    )
    grad = grad.astype(jnp.bfloat16).reshape(row_count, space_count, sub_rows)
    return (alpha, grad)


def solution(mesh):
    return jax.shard_map(
        per_device,
        mesh=mesh,
        in_specs=(P("space", None, "tm"), P("space", "tm"), P("tm", None), P(), P()),
        out_specs=(P("space", None, "tm"), P("space", None, "tm")),
        check_vma=False,
    )
```

profile of v0, /device:TPU:0, one launch (start us, length us, event | category | flops | bytes accessed | tf_op | source)
XLA Modules:
  0.0 778.3 jit_solution(7455162140651493963)
XLA Ops:
  7.2 0.0 copy-start
  7.2 0.0 all-gather.3.cloned.1.call-start
  7.2 0.7 all-gather.3.cloned.1.call-update
  7.9 0.0 all-reduce.3.cloned.1.call-start
  8.0 19.0 %all_gather.10 = bf16[512,512]{1,0:T(8,128)(2,1)S(1)} all-gather(bf16[128,512]{1,0:T(8,128)(2,1)} %param.7), channel_id=1, replica_groups=mesh['space'=8,'tm'=4] {'tm'}, dimensions={0}, use_global_device_ids=true | all-gather | bytes 655360 | tf_op jit(solution)/shard_map/all_gather | solution.py:27
  27.0 70.6 %all-gather.3.cloned.1.call-done = bf16[2048,2,512]{2,1,0:T(2,128)(2,1)} async-done(((bf16[2048,2,128]{2,1,0:T(2,128)(2,1)}), bf16[2048,2,512]{2,1,0:T(2,128)(2,1)}) %all-gather.3.cloned.1.call-update) | async-done | bytes 4194320 | tf_op jit(solution)/shard_map/all_gather | solution.py:26
  97.5 7.2 reshape.26
  104.7 6.5 convolution_convert_fusion.1
  111.2 7.1 reshape.27
  118.3 23.8 %convolution_bitcast_fusion = f32[4096,1024]{0,1:T(8,128)} fusion(bf16[2048,1024]{1,0:T(8,128)(2,1)} %reshape.27, bf16[2048,4096]{1,0:T(8,128)(2,1)} %param.6), kind=kOutput, calls=%fused_computation.2 | convolution fusion | flops 17179869184 | bytes 37748736 | tf_op jit(solution)/shard_map/dot_general | solution.py:34
  142.1 0.0 all-reduce.3.cloned.1.call-update
  142.2 0.0 all-gather.5.cloned.1.call-start
  142.2 0.0 copy-done
  142.2 0.7 dynamic_slice.6
  143.0 216.2 %all-reduce.3.cloned.1.call-done = f32[4096,1024]{0,1:T(8,128)} async-done(((f32[4096,1024]{0,1:T(8,128)}), f32[4096,1024]{0,1:T(8,128)}) %all-reduce.3.cloned.1.call-update) | async-done | bytes 16777232 | tf_op jit(solution)/shard_map/psum | solution.py:37
  359.2 26.6 %fusion.1 = f32[2048,1024]{0,1:T(8,128)} fusion(bf16[2048,4096]{1,0:T(8,128)(2,1)} %param.6, f32[4096,1024]{0,1:T(8,128)} %all-reduce.3.cloned.1.call-done, f32[1024]{0:T(1024)S(1)} %bitcast.21, f32[4096]{0:T(1024)S(1)} %dynamic_slice.6), kind=kOutput, calls=%fused_computation.7 | convolution fusion | flops 17196646400 | bytes 41963520 | tf_op jit(solution)/shard_map/dot_general | solution.py:40
  385.8 284.3 %all-reduce.4 = bf16[2048,1024]{0,1:T(8,128)(2,1)} all-reduce(f32[2048,1024]{0,1:T(8,128)} %fusion.1), channel_id=1, replica_groups=mesh['space'=8,'tm'=4] {'tm'}, use_global_device_ids=true, to_apply=%region_1.0 | all-reduce | flops 2097152 | bytes 12582912 | tf_op jit(solution)/shard_map/psum | solution.py:41
  670.1 2.3 constant_dynamic-slice_fusion
  672.4 0.0 all-gather.5.cloned.1.call-update
  672.4 0.0 copy-start.2
  672.4 6.4 copy.7
  678.9 7.2 reshape.28
  686.1 0.0 copy-done.2
  686.1 4.4 convolution_convert_fusion.2
  690.5 39.1 %all-gather.5.cloned.1.call-done = bf16[4096,1024]{0,1:T(8,128)(2,1)} async-done(((bf16[512,1024]{0,1:T(8,128)(2,1)}), bf16[4096,1024]{0,1:T(8,128)(2,1)}) %all-gather.5.cloned.1.call-update) | async-done | bytes 8388624 | tf_op jit(solution)/shard_map/all_gather | solution.py:57
  729.6 25.5 %convolution_convert_fusion = bf16[2048,4096]{1,0:T(8,128)(2,1)} fusion(bf16[4096,1024]{0,1:T(8,128)(2,1)} %all-gather.5.cloned.1.call-done, bf16[2048,1024]{0,1:T(8,128)(2,1)} %all-reduce.4, f32[1024]{0:T(1024)S(1)} %bitcast.22), kind=kOutput, calls=%fused_computation.1 | convolution fusion | flops 17196646400 | bytes 29364224 | tf_op jit(solution)/shard_map/dot_general | solution.py:55
  755.1 0.0 copy-start.1
  755.1 16.6 %copy.9 = bf16[256,8,8,512]{3,2,1,0:T(8,128)(2,1)} copy(bf16[256,8,8,512]{3,1,2,0:T(8,128)(2,1)} %bitcast.19) | data formatting | bytes 33554432
  771.8 0.0 copy-done.1
  (2 shorter events, 0.0 us)
Async XLA Ops:
  7.2 135.1 %copy-start = (f32[512]{0:T(512)S(1)}, f32[512]{0:T(512)}, u32[]{:S(2)}) copy-start(f32[512]{0:T(512)} %param.9) | copy-start | bytes 6148
  7.2 90.4 %all-gather.3.cloned.1.call-start = ((), (), s32[]{:S(2)}) async-start(), calls=%async_computation | async-start | bytes 5242880 | tf_op jit(solution)/shard_map/all_gather | solution.py:26
  7.9 351.3 %all-reduce.3.cloned.1.call-start = ((), (), s32[]{:S(2)}) async-start(), calls=%async_computation.1 | async-start | bytes 33554432 | tf_op jit(solution)/shard_map/psum | solution.py:37
  142.2 587.5 %all-gather.5.cloned.1.call-start = ((), (), s32[]{:S(2)}) async-start(), calls=%async_computation.2 | async-start | bytes 9437184 | tf_op jit(solution)/shard_map/all_gather | solution.py:57
  672.4 13.7 %copy-start.2 = (bf16[128,512]{1,0:T(8,128)(2,1)S(1)}, bf16[128,512]{1,0:T(8,128)(2,1)}, u32[]{:S(2)}) copy-start(bf16[128,512]{1,0:T(8,128)(2,1)} %param.7) | copy-start | bytes 393220
  755.1 16.6 %copy-start.1 = (f32[512]{0:T(512)S(1)}, f32[512]{0:T(512)}, u32[]{:S(2)}) copy-start(f32[512]{0:T(512)} %param.9) | copy-start | bytes 6148
Sparse Core Ops, SparseCore 0:
  9.5 87.9 all-gather.2
  142.3 216.8 all-reduce.2
  672.6 57.0 all-gather.4
where the time goes:
time: 779 us; the launch traced here: 778 us
  waiting for transfers between devices  327 us (42%)
  blocking collectives  303 us (39%)
  matrix products  86.8 us (11%)
  local copies, waits for them, and re-layouts  47.6 us (6%)
  between operations  13.8 us (2%)
    psum x1, blocking collectives, per_device(): back_all = lax.psum(back_part, 'tm').astype(jnp.bfloat16)  284 us
    psum x1, waiting for transfers between devices, per_device(): spectral = lax.psum(partial_spec, 'space')  216 us
    all_gather x1, waiting for transfers between devices, per_device(): lax.all_gather(series, 'tm', axis=2, tiled=True)  70.6 us
    all_gather x1, waiting for transfers between devices, per_device(): lax.all_gather(back_sub, 'space', axis=0, tiled=True)  39.1 us
    dot_general x1, matrix products, per_device(): jnp.dot(space_basis, scaled_spec, preferred_element_type=jnp.float32)  26.6 us
    dot_general x1, matrix products, per_device(): lax.dot_general(weighted, lax.all_gather(back_sub, 'space', axis=0, tiled...  25.5 us
    dot_general x1, matrix products, per_device(): lax.dot_general(space_basis, rotated, contract_rows, preferred_element_ty...  23.8 us
    all_gather x1, blocking collectives, per_device(): lax.all_gather(time_basis, 'tm', axis=0, tiled=True)  19 us
  transfers between devices with their start and end apart: 3, of which 3 were waited for; matrix products, arithmetic and copies ran while one was open for 2% of the time, Pallas kernels for 0%

commit v1 on v0

--- a/solution.py
+++ b/solution.py
@@ -5,6 +5,15 @@
 
 TIMES = 512
 REPS = 2
+
+
+def added_up(value, axis):
+    size = lax.axis_size(axis)
+    total, far = (value, 1)
+    while far < size:
+        total = total + lax.ppermute(total, axis, [(i, i ^ far) for i in range(size)])
+        far = 2 * far
+    return total
 
 
 def scale_block(spectral, eig_rows, eig_cols):
@@ -34,7 +43,7 @@
     partial_spec = lax.dot_general(
         space_basis, rotated, contract_rows, preferred_element_type=jnp.float32
     )
-    spectral = lax.psum(partial_spec, "space")
+    spectral = added_up(partial_spec, "space")
     eig_rows = lax.dynamic_slice_in_dim(space_eig, time_idx * col_block, col_block)
     scaled_spec = scale_block(spectral, eig_rows, cols_tiled)
     back_part = jnp.dot(space_basis, scaled_spec, preferred_element_type=jnp.float32)

time: 779 us -> 1330 us (1.71)
  waiting for transfers between devices: 327 us -> 847 us
  other arithmetic: 0 us -> 23.4 us
    ppermute x0 -> x3, waiting for transfers between devices: none -> 740 us  [added_up(): lax.ppermute(total, axis, [(i, i ^ far) for i in range(size)])]
    psum x1 -> x0, waiting for transfers between devices: 216 us -> none  [per_device(): spectral = lax.psum(partial_spec, 'space')]
    add x0 -> x2, other arithmetic: none -> 23.4 us  [added_up(): total + lax.ppermute(total, axis, [(i, i ^ far) for i in range(size)])]
  transfers between devices with their start and end apart: 3 -> 5, of which waited for: 3 -> 5; matrix products, arithmetic and copies ran while one was open for 2% -> 1% of each run, Pallas kernels for 0% -> 0%
where the time goes in v1:
time: 1330 us
  waiting for transfers between devices  847 us (64%)
  blocking collectives  301 us (23%)
  matrix products  85.5 us (6%)
  local copies, waits for them, and re-layouts  53.8 us (4%)
  other arithmetic  23.4 us (2%)
  between operations  14.1 us (1%)
    ppermute x3, waiting for transfers between devices, added_up(): lax.ppermute(total, axis, [(i, i ^ far) for i in range(size)])  740 us
    psum x1, blocking collectives, per_device(): back_all = lax.psum(back_part, 'tm').astype(jnp.bfloat16)  282 us
    all_gather x1, waiting for transfers between devices, per_device(): lax.all_gather(series, 'tm', axis=2, tiled=True)  70.6 us
    all_gather x1, waiting for transfers between devices, per_device(): lax.all_gather(back_sub, 'space', axis=0, tiled=True)  35.8 us
    dot_general x1, matrix products, per_device(): jnp.dot(space_basis, scaled_spec, preferred_element_type=jnp.float32)  26.7 us
  transfers between devices with their start and end apart: 5, of which 5 were waited for; matrix products, arithmetic and copies ran while one was open for 1% of the time, Pallas kernels for 0%

profile of v1, /device:TPU:0, one launch (start us, length us, event | category | flops | bytes accessed | tf_op | source)
XLA Modules:
  0.0 1327.4 jit_solution(1322161182806035810)
XLA Ops:
  7.2 0.0 copy-start
  7.2 0.0 all-gather.3.cloned.1.call-start
  7.2 0.7 all-gather.3.cloned.1.call-update
  7.9 0.0 all-gather.5.cloned.1.call-start
  8.0 19.0 %all_gather.10 = bf16[512,512]{1,0:T(8,128)(2,1)S(1)} all-gather(bf16[128,512]{1,0:T(8,128)(2,1)} %param.7), channel_id=1, replica_groups=mesh['space'=8,'tm'=4] {'tm'}, dimensions={0}, use_global_device_ids=true | all-gather | bytes 655360 | tf_op jit(solution)/shard_map/all_gather | solution.py:36
  27.0 70.6 %all-gather.3.cloned.1.call-done = bf16[2048,2,512]{2,1,0:T(2,128)(2,1)} async-done(((bf16[2048,2,128]{2,1,0:T(2,128)(2,1)}), bf16[2048,2,512]{2,1,0:T(2,128)(2,1)}) %all-gather.3.cloned.1.call-update) | async-done | bytes 4194320 | tf_op jit(solution)/shard_map/all_gather | solution.py:35
  97.5 7.2 reshape.26
  104.7 6.5 convolution_convert_fusion.1
  111.2 7.1 reshape.27
  118.3 22.5 %convolution_bitcast_fusion = f32[4096,1024]{0,1:T(8,128)S(1)} fusion(bf16[2048,1024]{1,0:T(8,128)(2,1)} %reshape.27, bf16[2048,4096]{1,0:T(8,128)(2,1)} %param.6), kind=kOutput, calls=%fused_computation.2 | convolution fusion | flops 17179869184 | bytes 37748736 | tf_op jit(solution)/shard_map/dot_general | solution.py:43
  140.7 0.0 copy-start.2
  140.8 0.1 collective-permute-start
  140.8 6.1 copy-done.2
  146.9 19.2 %collective-permute-done = f32[4096,1024]{0,1:T(8,128)} collective-permute-done((f32[4096,1024]{0,1:T(8,128)S(1)}, f32[4096,1024]{0,1:T(8,128)}, u32[]{:S(2)}, u32[]{:S(2)}) %collective-permute-start) | collective-permute-done | bytes 16777248 | tf_op jit(solution)/shard_map/ppermute | solution.py:14
  166.1 11.4 add.23
  177.5 1.5 collective-permute-start.1
  178.9 361.0 %collective-permute-done.1 = f32[4096,1024]{0,1:T(8,128)} collective-permute-done((f32[4096,1024]{0,1:T(8,128)S(1)}, f32[4096,1024]{0,1:T(8,128)}, u32[]{:S(2)}, u32[]{:S(2)}) %collective-permute-start.1) | collective-permute-done | bytes 16777248 | tf_op jit(solution)/shard_map/ppermute | solution.py:14
  539.9 12.1 add.24
  552.0 1.4 collective-permute-start.2
  553.3 0.0 copy-done
  553.3 0.7 dynamic_slice.6
  554.0 359.6 %collective-permute-done.2 = f32[4096,1024]{0,1:T(8,128)} collective-permute-done((f32[4096,1024]{0,1:T(8,128)}, f32[4096,1024]{0,1:T(8,128)}, u32[]{:S(2)}, u32[]{:S(2)}) %collective-permute-start.2) | collective-permute-done | bytes 16777248 | tf_op jit(solution)/shard_map/ppermute | solution.py:14
  913.7 26.7 %fusion.1 = f32[2048,1024]{0,1:T(8,128)} fusion(bf16[2048,4096]{1,0:T(8,128)(2,1)} %param.6, f32[4096,1024]{0,1:T(8,128)} %add.24, f32[4096,1024]{0,1:T(8,128)} %collective-permute-done.2, f32[1024]{0:T(1024)S(1)} %bitcast.21, f32[4096]{0:T(1024)S(1)} %dynamic_slice.6), kind=kOutput, calls=%fused_computation.7 | convolution fusion | flops 17200840704 | bytes 58740736 | tf_op jit(solution)/shard_map/dot_general | solution.py:49
  940.3 281.7 %all-reduce.1 = bf16[2048,1024]{0,1:T(8,128)(2,1)} all-reduce(f32[2048,1024]{0,1:T(8,128)} %fusion.1), channel_id=1, replica_groups=mesh['space'=8,'tm'=4] {'tm'}, use_global_device_ids=true, to_apply=%region_0.0 | all-reduce | flops 2097152 | bytes 12582912 | tf_op jit(solution)/shard_map/psum | solution.py:50
  1222.0 2.4 constant_dynamic-slice_fusion
  1224.4 0.0 all-gather.5.cloned.1.call-update
  1224.4 0.0 copy-start.3
  1224.4 6.5 copy.7
  1230.9 7.2 reshape.28
  1238.1 0.0 copy-done.3
  1238.1 4.4 convolution_convert_fusion.2
  1242.5 35.8 %all-gather.5.cloned.1.call-done = bf16[4096,1024]{0,1:T(8,128)(2,1)} async-done(((bf16[512,1024]{0,1:T(8,128)(2,1)}), bf16[4096,1024]{0,1:T(8,128)(2,1)}) %all-gather.5.cloned.1.call-update) | async-done | bytes 8388624 | tf_op jit(solution)/shard_map/all_gather | solution.py:66
  1278.4 25.5 %convolution_convert_fusion = bf16[2048,4096]{1,0:T(8,128)(2,1)} fusion(bf16[4096,1024]{0,1:T(8,128)(2,1)} %all-gather.5.cloned.1.call-done, bf16[2048,1024]{0,1:T(8,128)(2,1)} %all-reduce.1, f32[1024]{0:T(1024)S(1)} %bitcast.22), kind=kOutput, calls=%fused_computation.1 | convolution fusion | flops 17196646400 | bytes 29364224 | tf_op jit(solution)/shard_map/dot_general | solution.py:64
  1303.9 0.0 copy-start.1
  1303.9 16.6 %copy.9 = bf16[256,8,8,512]{3,2,1,0:T(8,128)(2,1)} copy(bf16[256,8,8,512]{3,1,2,0:T(8,128)(2,1)} %bitcast.19) | data formatting | bytes 33554432
  1320.5 0.0 copy-done.1
  (2 shorter events, 0.0 us)
Async XLA Ops:
  7.2 546.2 %copy-start = (f32[512]{0:T(512)S(1)}, f32[512]{0:T(512)}, u32[]{:S(2)}) copy-start(f32[512]{0:T(512)} %param.9) | copy-start | bytes 6148
  7.2 90.4 %all-gather.3.cloned.1.call-start = ((), (), s32[]{:S(2)}) async-start(), calls=%async_computation | async-start | bytes 5242880 | tf_op jit(solution)/shard_map/all_gather | solution.py:35
  7.9 1270.5 %all-gather.5.cloned.1.call-start = ((), (), s32[]{:S(2)}) async-start(), calls=%async_computation.1 | async-start | bytes 9437184 | tf_op jit(solution)/shard_map/all_gather | solution.py:66
  140.7 6.2 copy-start.2
  140.8 25.4 %collective-permute-start = (f32[4096,1024]{0,1:T(8,128)S(1)}, f32[4096,1024]{0,1:T(8,128)}, u32[]{:S(2)}, u32[]{:S(2)}) collective-permute-start(f32[4096,1024]{0,1:T(8,128)S(1)} %convolution_bitcast_fusion), channel_id=1, source_target_pairs={{0,4},{4,0},{8,12},{12,8},{16,20},{20,16},{24,28},{28,24},{1,5},{5... | collective-permute-start | bytes 50331656 | tf_op jit(solution)/shard_map/ppermute | solution.py:14
  177.5 362.4 %collective-permute-start.1 = (f32[4096,1024]{0,1:T(8,128)S(1)}, f32[4096,1024]{0,1:T(8,128)}, u32[]{:S(2)}, u32[]{:S(2)}) collective-permute-start(f32[4096,1024]{0,1:T(8,128)S(1)} %add.23), channel_id=1, source_target_pairs={{0,8},{4,12},{8,0},{12,4},{16,24},{20,28},{24,16},{28,20},{1,9},{5... | collective-permute-start | bytes 50331656 | tf_op jit(solution)/shard_map/ppermute | solution.py:14
  552.0 361.7 %collective-permute-start.2 = (f32[4096,1024]{0,1:T(8,128)}, f32[4096,1024]{0,1:T(8,128)}, u32[]{:S(2)}, u32[]{:S(2)}) collective-permute-start(f32[4096,1024]{0,1:T(8,128)} %add.24), channel_id=1, source_target_pairs={{0,16},{4,20},{8,24},{12,28},{16,0},{20,4},{24,8},{28,12},{1,17},{... | collective-permute-start | bytes 50331656 | tf_op jit(solution)/shard_map/ppermute | solution.py:14
  1224.4 13.7 %copy-start.3 = (bf16[128,512]{1,0:T(8,128)(2,1)S(1)}, bf16[128,512]{1,0:T(8,128)(2,1)}, u32[]{:S(2)}) copy-start(bf16[128,512]{1,0:T(8,128)(2,1)} %param.7) | copy-start | bytes 393220
  1303.9 16.6 %copy-start.1 = (f32[512]{0:T(512)S(1)}, f32[512]{0:T(512)}, u32[]{:S(2)}) copy-start(f32[512]{0:T(512)} %param.9) | copy-start | bytes 6148
Sparse Core Ops, SparseCore 0:
  9.5 87.9 all-gather.2
  1224.5 53.7 all-gather.4
